TPU v7x, 32 devices: a whole 2x2x4 slice. The times are simulated.
32 devices in a mesh: dp: 4 (over z), tensor: 8 (over y, x, core).
Axes of the slice: x: 2, y: 2, z: 4, core: 2. Of those that a mesh axis runs over, the one named last changes fastest.
Arguments:
- tokens: bfloat16 [8192, 1152], P('dp'), may hold values from -6 to 6
- condition: float32 [32, 1152], P('dp'), may hold values from -6 to 6
- timesteps: int32 [32], P('dp'), may hold values from 0 to 999
- route_masks: int32 [1000, 16, 2], P(None, 'tensor'), may hold values 0 or 1
- modulate_weight: bfloat16 [1152, 6, 1152], P(None, None, 'tensor'), may hold values from -0.1875 to 0.1875
- modulate_bias: bfloat16 [6, 1152], P(None, 'tensor'), may hold values from -1.5 to 1.5
- input_weight: bfloat16 [1152, 3, 1152], P(None, None, 'tensor'), may hold values from -0.1875 to 0.1875
- input_bias: bfloat16 [2, 1152], P(None, 'tensor'), may hold values from -1.5 to 1.5
- output_weight: bfloat16 [1152, 1152], P('tensor'), may hold values from -1.5 to 1.5
- output_bias: bfloat16 [1152], replicated, may hold values from -1.5 to 1.5
- expand_weight: bfloat16 [1152, 4608], P(None, 'tensor'), may hold values from -0.1875 to 0.1875
- expand_bias: bfloat16 [4608], P('tensor'), may hold values from -1.5 to 1.5
- reduce_weight: bfloat16 [4608, 1152], P('tensor'), may hold values from -0.1875 to 0.1875
- reduce_bias: bfloat16 [1152], replicated, may hold values from -1.5 to 1.5
- router_weight: bfloat16 [1152, 16, 2], P(None, 'tensor'), may hold values from -0.1875 to 0.1875
- router_bias: bfloat16 [16, 2], P('tensor'), may hold values from -1.2 to 1.2
- out_cotangent: bfloat16 [8192, 1152], P('dp'), may hold values from -6 to 6
Outputs:
- block_output: float32 [8192, 1152], P('dp')
- tokens_grad: float32 [8192, 1152], P('dp')
- modulate_weight_grad: float32 [1152, 6, 1152], P(None, None, 'tensor')
- modulate_bias_grad: float32 [6, 1152], P(None, 'tensor')
- input_weight_grad: float32 [1152, 3, 1152], P(None, None, 'tensor')
- input_bias_grad: float32 [2, 1152], P(None, 'tensor')
- output_weight_grad: float32 [1152, 1152], P('tensor')
- output_bias_grad: float32 [1152], replicated
- expand_weight_grad: float32 [1152, 4608], P(None, 'tensor')
- expand_bias_grad: float32 [4608], P('tensor')
- reduce_weight_grad: float32 [4608, 1152], P('tensor')
- reduce_bias_grad: float32 [1152], replicated
- router_weight_grad: float32 [1152, 16, 2], P(None, 'tensor')
- router_bias_grad: float32 [16, 2], P('tensor')
Inputs may be any that keep to these rules, and one draw needn't show every extreme that they name: `timesteps`: each timestep selects the row of route_masks used by its item.
All inputs are finite; a program needn't handle non-finite values. No bound on the sum of `route_masks` on one device may be relied on, other than what follows from the above.
Results may differ from a plain program's by a relative error of at most 0.013.
The roundings to bfloat16 on the way count: a program that leaves them out, or rounds other values in their place, can miss the bound.
Values may be sent and summed in bfloat16 or wider, within the bound.
A program may use at most 256 MiB of HBM per device.

v0:
```python
import math
import jax
import jax.numpy as jnp
from jax import lax
from jax.sharding import PartitionSpec as P

HIGHEST = lax.Precision.HIGHEST
EPSILON = 1e-06


def layer_norm(values):
    center = values - jnp.mean(values, axis=-1, keepdims=True)
    inverse = lax.rsqrt(jnp.mean(center * center, axis=-1, keepdims=True) + EPSILON)
    return (center * inverse, inverse)


def norm_back(grad_norm, normed, inverse):
    mean_grad = jnp.mean(grad_norm, axis=-1, keepdims=True)
    mean_cross = jnp.mean(grad_norm * normed, axis=-1, keepdims=True)
    return inverse * (grad_norm - mean_grad - normed * mean_cross)


def gelu_tanh(values):
    return jax.nn.gelu(values, approximate=True)


def contract_rows(left, right):
    return lax.dot_general(
        left, right, (((0,), (0,)), ((), ())), preferred_element_type=jnp.float32
    )


def contract_cols(left, right):
    return lax.dot_general(
        left, right, (((1,), (1,)), ((), ())), preferred_element_type=jnp.float32
    )


def body(
    tokens,
    condition,
    timesteps,
    route_masks,
    modulate_weight,
    modulate_bias,
    input_weight,
    input_bias,
    output_weight,
    output_bias,
    expand_weight,
    expand_bias,
    reduce_weight,
    reduce_bias,
    router_weight,
    router_bias,
    out_cotangent,
):
    model_width = tokens.shape[1]
    item_count = condition.shape[0]
    rows_all = tokens.shape[0]
    item_length = rows_all // item_count
    local_heads = router_weight.shape[1]
    local_width = input_weight.shape[2]
    head_size = local_width // local_heads
    group_width = expand_weight.shape[1] // local_heads
    score_scale = 1.0 / math.sqrt(head_size)
    silu_condition = jax.nn.silu(condition).astype(jnp.bfloat16)
    condition_low = condition.astype(jnp.bfloat16)
    modulate_part = jnp.einsum(
        "bd,dke->bke", silu_condition, modulate_weight, preferred_element_type=jnp.float32
    ) + modulate_bias.astype(jnp.float32)
    modulation = lax.all_gather(modulate_part, "tensor", axis=2, tiled=True)
    shift_one, scale_one, gate_one, shift_two, scale_two, gate_two = [
        modulation[:, column][:, None, :] for column in range(6)
    ]
    logits = jnp.einsum(
        "bd,dhc->bhc", condition_low, router_weight, preferred_element_type=jnp.float32
    ) + router_bias.astype(jnp.float32)
    sigmoid_out = jax.nn.sigmoid(logits)
    step_table = (
        timesteps[:, None] == jnp.arange(route_masks.shape[0], dtype=jnp.int32)[None, :]
    ).astype(jnp.float32)
    mask_rows = jnp.einsum(
        "bs,shc->bhc", step_table, route_masks.astype(jnp.float32), precision=HIGHEST
    )
    gate_values = mask_rows * sigmoid_out
    head_gate = gate_values[:, :, 0]
    group_gate = gate_values[:, :, 1]
    inputs_f = tokens.astype(jnp.float32).reshape(item_count, item_length, model_width)
    normed_one, inverse_one = layer_norm(inputs_f)
    hidden_one = (normed_one * (1.0 + scale_one) + shift_one).astype(jnp.bfloat16)
    projected = jnp.einsum(
        "bsd,dke->bske", hidden_one, input_weight, preferred_element_type=jnp.float32
    )
    input_bias_f = input_bias.astype(jnp.float32)
    head_shape = (item_count, item_length, local_heads, head_size)
    queries = (projected[:, :, 0] + input_bias_f[0]).astype(jnp.bfloat16).reshape(head_shape)
    keys_low = projected[:, :, 1].astype(jnp.bfloat16).reshape(head_shape)
    values_low = (projected[:, :, 2] + input_bias_f[1]).astype(jnp.bfloat16).reshape(head_shape)
    scores = (
        jnp.einsum("bqhe,bkhe->bhqk", queries, keys_low, preferred_element_type=jnp.float32)
        * score_scale
    )
    row_max = jnp.max(scores, axis=-1, keepdims=True)
    log_total = row_max + jnp.log(jnp.sum(jnp.exp(scores - row_max), axis=-1, keepdims=True))
    softmax_low = jnp.exp(scores - log_total).astype(jnp.bfloat16)
    mixed_heads = jnp.einsum(
        "bhqk,bkhe->bqhe", softmax_low, values_low, preferred_element_type=jnp.float32
    )
    gated_heads = (
        (mixed_heads * head_gate[:, None, :, None])
        .astype(jnp.bfloat16)
        .reshape(rows_all, local_width)
    )
    attention_part = jnp.dot(gated_heads, output_weight, preferred_element_type=jnp.float32)
    attention = (lax.psum(attention_part, "tensor") + output_bias.astype(jnp.float32)).reshape(
        item_count, item_length, model_width
    )
    residual_one = inputs_f + gate_one * attention
    normed_two, inverse_two = layer_norm(residual_one)
    hidden_two = (
        (normed_two * (1.0 + scale_two) + shift_two)
        .astype(jnp.bfloat16)
        .reshape(rows_all, model_width)
    )
    expanded = jnp.dot(
        hidden_two, expand_weight, preferred_element_type=jnp.float32
    ) + expand_bias.astype(jnp.float32)
    activated = gelu_tanh(expanded)
    group_shape = (item_count, item_length, local_heads, group_width)
    gated_channels = (
        (activated.reshape(group_shape) * group_gate[:, None, :, None])
        .astype(jnp.bfloat16)
        .reshape(rows_all, -1)
    )
    mlp_part = jnp.dot(gated_channels, reduce_weight, preferred_element_type=jnp.float32)
    branch_two = (lax.psum(mlp_part, "tensor") + reduce_bias.astype(jnp.float32)).reshape(
        item_count, item_length, model_width
    )
    block_output = residual_one + gate_two * branch_two
    cotangent = out_cotangent.astype(jnp.float32).reshape(item_count, item_length, model_width)
    gate_two_grad = jnp.sum(cotangent * branch_two, axis=1)
    branch_grad = (gate_two * cotangent).astype(jnp.bfloat16).reshape(rows_all, model_width)
    reduce_bias_grad = jnp.sum(branch_grad.astype(jnp.float32), axis=0)
    reduce_weight_grad = contract_rows(gated_channels, branch_grad)
    channel_blocks = contract_cols(branch_grad, reduce_weight).reshape(group_shape)
    group_gate_grad = jnp.sum(channel_blocks * activated.reshape(group_shape), axis=(1, 3))
    activated_grad = (channel_blocks * group_gate[:, None, :, None]).reshape(rows_all, -1)
    expanded_grad = jax.vjp(gelu_tanh, expanded)[1](activated_grad)[0].astype(jnp.bfloat16)
    expand_bias_grad = jnp.sum(expanded_grad.astype(jnp.float32), axis=0)
    expand_weight_grad = contract_rows(hidden_two, expanded_grad)
    hidden_two_part = contract_cols(expanded_grad, expand_weight)
    hidden_two_grad = lax.psum(hidden_two_part, "tensor").reshape(
        item_count, item_length, model_width
    )
    shift_two_grad = jnp.sum(hidden_two_grad, axis=1)
    scale_two_grad = jnp.sum(hidden_two_grad * normed_two, axis=1)
    residual_grad = cotangent + norm_back(
        hidden_two_grad * (1.0 + scale_two), normed_two, inverse_two
    )
    branch_one_grad = (gate_one * residual_grad).astype(jnp.bfloat16).reshape(rows_all, model_width)
    output_bias_grad = jnp.sum(branch_one_grad.astype(jnp.float32), axis=0)
    output_weight_grad = contract_rows(gated_heads, branch_one_grad)
    heads_grad = contract_cols(branch_one_grad, output_weight).reshape(head_shape)
    head_gate_grad = jnp.sum(heads_grad * mixed_heads, axis=(1, 3))
    mixed_grad = (heads_grad * head_gate[:, None, :, None]).astype(jnp.bfloat16)
    scores_again = (
        jnp.einsum("bqhe,bkhe->bhqk", queries, keys_low, preferred_element_type=jnp.float32)
        * score_scale
    )
    softmax_full = jnp.exp(scores_again - log_total)
    softmax_grad = jnp.einsum(
        "bqhe,bkhe->bhqk", mixed_grad, values_low, preferred_element_type=jnp.float32
    )
    values_grad = jnp.einsum(
        "bhqk,bqhe->bkhe",
        softmax_full.astype(jnp.bfloat16),
        mixed_grad,
        preferred_element_type=jnp.float32,
    )
    score_grad = (
        softmax_full * (softmax_grad - jnp.sum(softmax_grad * softmax_full, axis=-1, keepdims=True))
    ).astype(jnp.bfloat16)
    queries_grad = (
        jnp.einsum("bhqk,bkhe->bqhe", score_grad, keys_low, preferred_element_type=jnp.float32)
        * score_scale
    )
    keys_grad = (
        jnp.einsum("bhqk,bqhe->bkhe", score_grad, queries, preferred_element_type=jnp.float32)
        * score_scale
    )
    stacked_grad = (
        jnp.stack([queries_grad, keys_grad, values_grad], axis=2)
        .reshape(item_count, item_length, 3, local_width)
        .astype(jnp.bfloat16)
    )
    stacked_f = stacked_grad.astype(jnp.float32)
    input_bias_grad = jnp.stack(
        [jnp.sum(stacked_f[:, :, 0], axis=(0, 1)), jnp.sum(stacked_f[:, :, 2], axis=(0, 1))]
    )
    input_weight_grad = jnp.einsum(
        "bsd,bske->dke", hidden_one, stacked_grad, preferred_element_type=jnp.float32
    )
    hidden_one_part = jnp.einsum(
        "bske,dke->bsd", stacked_grad, input_weight, preferred_element_type=jnp.float32
    ).reshape(rows_all, model_width)
    hidden_one_grad = lax.psum(hidden_one_part, "tensor")
    gate_one_grad = jnp.sum(residual_grad * attention, axis=1)
    hidden_one_grad = hidden_one_grad.reshape(item_count, item_length, model_width)
    shift_one_grad = jnp.sum(hidden_one_grad, axis=1)
    scale_one_grad = jnp.sum(hidden_one_grad * normed_one, axis=1)
    tokens_grad = residual_grad + norm_back(
        hidden_one_grad * (1.0 + scale_one), normed_one, inverse_one
    )
    modulation_grad = jnp.stack(
        [
            shift_one_grad,
            scale_one_grad,
            gate_one_grad,
            shift_two_grad,
            scale_two_grad,
            gate_two_grad,
        ],
        axis=1,
    )
    column_start = lax.axis_index("tensor") * modulate_weight.shape[2]
    own_grad = lax.dynamic_slice_in_dim(modulation_grad, column_start, modulate_weight.shape[2], 2)
    modulate_weight_grad = jnp.einsum(
        "bd,bke->dke", silu_condition.astype(jnp.float32), own_grad, precision=HIGHEST
    )
    modulate_bias_grad = jnp.sum(own_grad, axis=0)
    gate_grad = jnp.stack([head_gate_grad, group_gate_grad], axis=-1)
    logit_grad = gate_grad * mask_rows * sigmoid_out * (1.0 - sigmoid_out)
    router_weight_grad = jnp.einsum(
        "bd,bhc->dhc", condition_low.astype(jnp.float32), logit_grad, precision=HIGHEST
    )
    router_bias_grad = jnp.sum(logit_grad, axis=0)
    summed = lax.psum(
        (
            modulate_weight_grad,
            modulate_bias_grad,
            input_weight_grad,
            input_bias_grad,
            output_weight_grad,
            output_bias_grad,
            expand_weight_grad,
            expand_bias_grad,
            reduce_weight_grad,
            reduce_bias_grad,
            router_weight_grad,
            router_bias_grad,
        ),
        "dp",
    )
    return (
        block_output.reshape(rows_all, model_width),
        tokens_grad.reshape(rows_all, model_width),
    ) + tuple(summed)


def solution(mesh):
    return jax.shard_map(
        body,
        mesh=mesh,
        in_specs=(
            P("dp", None),
            P("dp", None),
            P("dp"),
            P(None, "tensor", None),
            P(None, None, "tensor"),
            P(None, "tensor"),
            P(None, None, "tensor"),
            P(None, "tensor"),
            P("tensor", None),
            P(),
            P(None, "tensor"),
            P("tensor"),
            P("tensor", None),
            P(),
            P(None, "tensor", None),
            P("tensor", None),
            P("dp", None),
        ),
        out_specs=(
            P("dp", None),
            P("dp", None),
            P(None, None, "tensor"),
            P(None, "tensor"),
            P(None, None, "tensor"),
            P(None, "tensor"),
            P("tensor", None),
            P(),
            P(None, "tensor"),
            P("tensor"),
            P("tensor", None),
            P(),
            P(None, "tensor", None),
            P("tensor", None),
        ),
        check_vma=False,
    )
```

profile of v0, /device:TPU:0, one launch (start us, length us, event | category | flops | bytes accessed | tf_op | source)
XLA Modules:
  0.0 1134.2 jit_solution(17159783250025493048)
XLA Ops:
  7.3 3.2 convert_reduce_fusion.2
  10.5 3.7 multiply_reduce_fusion.5
  14.2 0.6 copy-done.29
  14.8 0.7 convolution_add_fusion
  15.8 29.1 %all_gather.3 = f32[8,6,1152]{1,0,2:T(8,128)} all-gather(f32[8,6,144]{1,0,2:T(8,128)S(1)} %copy.78), channel_id=1, replica_groups=mesh['dp'=4,'tensor'=8] {'tensor'}, dimensions={2}, use_global_device_ids=true | all-gather | bytes 248832 | tf_op jit(solution)/shard_map/all_gather | solution.py:72
  44.9 22.1 %fusion.64 = (f32[8,1,1152]{1,0,2:T(8,128)}, f32[8,1,1152]{1,0,2:T(8,128)}, f32[8,1,1152]{1,0,2:T(8,128)}, f32[8,1,1152]{1,0,2:T(8,128)}, f32[8,1,1152]{1,0,2:T(8,128)}, /*index=5*/f32[8,1,1152]{1,0,2:T(8,128)}) fusion(f32[8,6,1152]{1,0,2:T(8,128)} %all_gather.3), kind=kLoop, calls=%fused_computation.135 | loop fusion | bytes 442368 | tf_op jit(solution)/shard_map/slice | solution.py:74
  67.0 3.4 copy.114
  70.4 3.3 copy.113
  73.8 4.9 fusion.17
  79.8 0.8 fusion.67
  80.7 0.8 multiply_reduce_fusion.7
  81.5 0.8 exponential_reduce_fusion
  82.3 2.0 multiply_convert_fusion.3
  84.7 5.3 fusion.70
  91.1 4.4 copy.121
  95.5 3.6 copy.116
  99.2 3.3 copy.115
  102.5 3.4 copy.112
  105.9 3.4 copy.117
  109.3 4.5 convert_reduce_fusion
  113.9 5.1 broadcast_multiply_fusion
  119.0 2.7 copy.90
  121.7 4.4 copy.122
  126.1 102.3 %all-reduce.8.cloned.1.call-done = f32[2048,1152]{1,0:T(8,128)} async-done(((f32[2048,1152]{1,0:T(8,128)}), f32[2048,1152]{1,0:T(8,128)}) %all-reduce.8.cloned.1.call-update) | async-done | bytes 9437200 | tf_op jit(solution)/shard_map/psum | solution.py:116
  228.4 10.4 fusion.62
  238.8 4.9 multiply_reduce_fusion.4
  243.7 1.4 copy-done.2
  245.1 2.2 fusion.5
  248.4 8.9 multiply_convert_fusion
  257.2 1.4 copy-done.55
  258.6 7.0 fusion.72
  265.7 9.8 fusion.71
  275.6 128.3 %all-reduce.10.cloned.1.call-done = f32[2048,1152]{1,0:T(8,128)} async-done(((f32[2048,1152]{1,0:T(8,128)}), f32[2048,1152]{1,0:T(8,128)}) %all-reduce.10.cloned.1.call-update) | async-done | bytes 9437200 | tf_op jit(solution)/shard_map/psum | solution.py:153
  403.8 8.1 fusion.9
  411.9 1.0 copy-done.5
  412.9 10.7 convert_reduce_fusion.1
  423.6 2.6 multiply_reduce_fusion.8
  426.2 1.3 copy-done.4
  427.5 1.0 convolution_convert_fusion
  428.5 1.3 multiply_reduce_fusion.6
  429.9 1.2 multiply_convert_fusion.1
  431.0 0.8 fusion.27
  432.4 2.1 fusion.55
  434.7 5.4 convolution_bitcast_fusion
  440.8 7.9 fusion.75
  448.7 4.7 fusion.74
  453.5 4.3 fusion.73
  457.8 6.6 fusion.22
  464.4 215.9 %all-reduce.12.cloned.1.call-done = (f32[2048,1152]{1,0:T(8,128)}, f32[2048,1152]{1,0:T(8,128)}) async-done(((f32[2048,1152]{1,0:T(8,128)}, f32[2048,1152]{1,0:T(8,128)}), (f32[2048,1152]{1,0:T(8,128)}, f32[2048,1152]{1,0:T(8,128)})) %all-reduce.12.cloned.1.call-update) | async-done | bytes 18874384 | tf_op jit(solution)/shard_map/psum | solution.py:137
  680.3 22.4 %fusion.7 = (f32[8,1152]{1,0:T(8,128)S(1)}, f32[8,1152]{1,0:T(8,128)S(1)}, f32[8,1152]{1,0:T(8,128)S(1)}, f32[8,1152]{1,0:T(8,128)S(1)}, f32[8,1152]{1,0:T(8,128...) fusion(f32[2048,1152]{1,0:T(8,128)} %all-reduce.10.cloned.1.call-done, f32[2048,1152]{1,0:T(8,128)} %all-reduce.8.cloned.1.call-done, ...), kind=kLoop, calls=%fused_computation.17 | loop fusion | flops 61286400 | bytes 56976384 | tf_op jit(solution)/shard_map/reduce_sum | solution.py:157
  702.7 3.8 fusion.37
  706.6 4.6 copy.123
  711.2 5.8 fusion.21
  717.2 1.8 slice_reduce_fusion.1
  719.3 7.0 fusion.8
  726.3 11.0 fusion.2
  737.4 11.9 %multiply_add_fusion = f32[2048,1152]{1,0:T(8,128)} fusion(f32[2048,1152]{1,0:T(8,128)} %get-tuple-element.52, f32[2048,1152]{1,0:T(8,128)} %get-tuple-element.31, bf16[2048,1152]{1,0:T(8,128)(2,1)} %param.17, f32[2048]{0:T(1024)S(1)} %broadcast_multiply_fusion.1, f32[2048]{0:T(1024)S(1)} %broadcast_multiply_fusion.2, f32[2048]{0:T(1024)S(1)} %copy-done.30, ...), kind=kLoop, calls=%fused_computation.24 | loop fusion | flops 21233664 | bytes 33099776 | tf_op jit(solution)/shard_map/add | solution.py:212
  749.4 26.8 %all-reduce.1 = (f32[6,144]{1,0:T(8,128)}, f32[2,144]{1,0:T(2,128)}, f32[1152]{0:T(1024)}, f32[576]{0:T(1024)}, f32[1152]{0:T(1024)}, /*index=5*/f32[1152,2,2]{0,2,1:T(2,128)}, f32[2,2]{1,0:T(2,128)}) all-reduce(f32[6,144]{1,0:T(8,128)S(1)} %dynamic-slice_reduce_fusion, ...), channel_id=1, replica_groups=mesh['dp'=4,'tensor'=8] {'dp'}, use_global_device_ids=true, to_apply=%region_23.24 | all-reduce | flops 8644 | bytes 69152 | tf_op jit(solution)/shard_map/psum | solution.py:238
  776.2 341.5 %all-reduce.14.cloned.1.call-done = (f32[1152,6,144]{0,2,1:T(8,128)}, f32[1152,3,144]{0,2,1:T(8,128)}, f32[144,1152]{1,0:T(8,128)}, f32[1152,576]{0,1:T(8,128)}, f32[576,1152]{1,0:T(8,128)}) async-done(((f32[1152,6,144]{0,2,1:T(8,128)}, f32[1152,3,144]{0,2,1:T(8,128)}, f32[144,1152]{1,0:T(8,128)}, f32[1152,576]{0,1:T(8,128)}, f32[576,1152]{1,0:T(8,128)}), (f32[1152,6,144]{0,2,1:T(8,128)}, ...) | async-done | bytes 11943952 | tf_op jit(solution)/shard_map/psum | solution.py:238
  1117.7 4.5 copy.141
  1122.2 1.3 copy.142
  1123.5 0.8 copy.143
  1124.3 1.5 copy.144
  1125.8 1.5 copy.145
  (179 shorter events, 6.2 us)
Async XLA Ops:
  7.2 7.6 copy-start
  7.2 7.0 copy-start.37
  7.2 7.6 copy-start.25
  7.2 221.2 %all-reduce.8.cloned.1.call-start = ((), (), s32[]{:S(2)}) async-start(), calls=%async_computation | async-start | bytes 18874368 | tf_op jit(solution)/shard_map/psum | solution.py:116
  10.4 34.5 %copy-start.27 = (f32[2048]{0:T(1024)}, f32[2048]{0:T(1024)S(1)}, u32[]{:S(2)}) copy-start(f32[2048]{0:T(1024)S(1)} %broadcast_multiply_fusion.6) | copy-start | bytes 24580
  67.0 6.8 copy-start.48
  78.7 0.7 copy-start.45
  78.7 0.9 copy-start.51
  78.7 1.0 copy-start.50
  78.7 1.0 copy-start.53
  78.8 2.7 copy-start.9
  79.5 2.8 copy-start.35
  79.6 2.7 copy-start.33
  79.7 0.8 copy-start.42
  81.5 2.8 copy-start.3
  82.3 2.4 copy-start.21
  84.6 5.4 copy-start.7
  90.0 0.7 copy-start.41
  90.0 0.8 copy-start.38
  90.0 313.8 %all-reduce.10.cloned.1.call-start = ((), (), s32[]{:S(2)}) async-start(), calls=%async_computation.1 | async-start | bytes 18874368 | tf_op jit(solution)/shard_map/psum | solution.py:153
  102.5 6.8 copy-start.23
  109.3 4.6 copy-start.47
  113.9 5.1 copy-start.11
  238.7 6.4 copy-start.2
  238.8 8.6 slice-start.2
  238.8 8.7 slice-start.4
  245.1 2.7 slice-start.3
  245.1 2.8 slice-start.5
  245.1 3.2 copy-start.46
  247.3 9.9 copy-start.13
  257.2 1.4 copy-start.55
  265.7 414.6 %all-reduce.12.cloned.1.call-start = ((), (), s32[]{:S(2)}) async-start(), calls=%async_computation.2 | async-start | bytes 37748736 | tf_op jit(solution)/shard_map/psum | solution.py:137
  403.8 9.1 copy-start.5
  412.9 10.7 copy-start.12
  423.6 4.9 copy-start.6
  423.6 3.9 copy-start.4
  426.2 2.3 copy-start.36
  428.5 3.9 copy-start.16
  429.9 1.2 copy-start.34
  429.9 2.0 copy-start.10
  431.8 2.6 copy-start.18
  432.4 2.3 copy-start.49
  440.1 0.7 copy-start.39
  440.1 8.6 slice-start
  440.1 677.6 %all-reduce.14.cloned.1.call-start = ((), (), s32[]{:S(2)}) async-start(), calls=%async_computation.3 | async-start | bytes 23887872 | tf_op jit(solution)/shard_map/psum | solution.py:238
  440.8 7.9 slice-start.1
  440.8 7.9 copy-start.54
  448.7 4.8 copy-start.8
  453.5 4.3 copy-start.17
  453.5 4.3 copy-start.19
  680.3 22.5 %copy-start.26 = (f32[8,1152]{1,0:T(8,128)S(1)}, f32[8,1152]{1,0:T(8,128)}, u32[]{:S(2)}) copy-start(f32[8,1152]{1,0:T(8,128)} %param.18) | copy-start | bytes 110596
  711.1 6.0 copy-start.32
  711.1 7.9 copy-start.43
  711.1 7.9 copy-start.44
  711.2 8.1 copy-start.28
  711.2 8.1 copy-start.30
  719.3 7.0 copy-start.24
  737.3 12.0 %copy-start.31 = (f32[1152]{0:T(1024)S(1)}, f32[1152]{0:T(1024)}, u32[]{:S(2)}) copy-start(f32[1152]{0:T(1024)} %get-tuple-element.46) | copy-start | bytes 13828
  737.3 12.0 %copy-start.40 = (f32[576]{0:T(1024)S(1)}, f32[576]{0:T(1024)}, u32[]{:S(2)}) copy-start(f32[576]{0:T(1024)} %get-tuple-element.58) | copy-start | bytes 6916
  1117.7 4.5 copy-start.20
  1117.7 5.8 copy-start.22
  1117.7 6.6 copy-start.15
  1122.2 3.6 copy-start.14
  1123.5 3.9 copy-start.1
  (2 other events, 1.3 us)
Sparse Core Ops, SparseCore 0:
  90.1 138.1 all-reduce.7
  265.8 137.9 all-reduce.9
  440.2 240.0 all-reduce.11
  706.7 410.9 all-reduce.13
where the time goes:
time: 1140 us; the launch traced here: 1130 us
  waiting for transfers between devices  788 us (69%)
  other arithmetic  112 us (10%)
  matrix products  84.5 us (7%)
  local copies, waits for them, and re-layouts  78.5 us (7%)
  blocking collectives  55.9 us (5%)
  between operations  14.9 us (1%)
    psum x1, waiting for transfers between devices, body(): lax.psum((modulate_weight_grad, modulate_bias_grad, input_weight_grad, in...  341 us
    psum x1, waiting for transfers between devices, body(): lax.psum(mlp_part, 'tensor') + reduce_bias.astype(jnp.float32)  216 us
    psum x1, waiting for transfers between devices, body(): lax.psum(hidden_two_part, 'tensor')  128 us
    psum x1, waiting for transfers between devices, body(): lax.psum(attention_part, 'tensor') + output_bias.astype(jnp.float32)  102 us
    unnamed x144, local copies, waits for them, and re-layouts  51.7 us
    all_gather x1, blocking collectives, body(): modulation = lax.all_gather(modulate_part, 'tensor', axis=2, tiled=True)  29.1 us
    psum x1, blocking collectives, body(): lax.psum((modulate_weight_grad, modulate_bias_grad, input_weight_grad, in...  26.8 us
  transfers between devices with their start and end apart: 4, of which 4 were waited for; matrix products, arithmetic and copies ran while one was open for 10% of the time, Pallas kernels for 0%

commit v1 on v0

--- a/solution.py
+++ b/solution.py
@@ -69,7 +69,15 @@
     modulate_part = jnp.einsum(
         "bd,dke->bke", silu_condition, modulate_weight, preferred_element_type=jnp.float32
     ) + modulate_bias.astype(jnp.float32)
-    modulation = lax.all_gather(modulate_part, "tensor", axis=2, tiled=True)
+    ways, here, step = (lax.axis_size("tensor"), lax.axis_index("tensor"), modulate_part.shape[2])
+    line, have = (modulate_part, 1)
+    while have < ways:
+        line = jnp.concatenate(
+            [line, lax.ppermute(line, "tensor", [(d, (d - have) % ways) for d in range(ways)])],
+            axis=2,
+        )
+        have = 2 * have
+    modulation = jnp.roll(line, here * step, axis=2)
     shift_one, scale_one, gate_one, shift_two, scale_two, gate_two = [
         modulation[:, column][:, None, :] for column in range(6)
     ]

time: 1140 us -> 1100 us (0.965)
  local copies, waits for them, and re-layouts: 78.5 us -> 40.6 us
  blocking collectives: 55.9 us -> 24.9 us
  waiting for transfers between devices: 788 us -> 818 us
  other arithmetic: 112 us -> 100 us
    all_gather x1 -> x0, blocking collectives: 29.1 us -> none  [body(): modulation = lax.all_gather(modulate_part, 'tensor', axis=2, tiled=True)]
    slice x1 -> x0, local copies, waits for them, and re-layouts: 22.1 us -> none  [body(): modulation[:, column][:, None, :]]
    psum x1, waiting for transfers between devices: 102 us -> 119 us  [body(): lax.psum(attention_part, 'tensor') + output_bias.astype(jnp.float32)]
    unnamed x144 -> x160, local copies, waits for them, and re-layouts: 51.7 us -> 36.1 us
  transfers between devices with their start and end apart: 4 -> 7, of which waited for: 4 -> 6; matrix products, arithmetic and copies ran while one was open for 10% -> 9% of each run, Pallas kernels for 0% -> 0%
where the time goes in v1:
time: 1100 us; the launch traced here: 1090 us
  waiting for transfers between devices  818 us (74%)
  other arithmetic  100 us (9%)
  matrix products  85.4 us (8%)
  local copies, waits for them, and re-layouts  40.6 us (4%)
  blocking collectives  24.9 us (2%)
  between operations  15.1 us (1%)
    psum x1, waiting for transfers between devices, body(): lax.psum((modulate_weight_grad, modulate_bias_grad, input_weight_grad, in...  347 us
    psum x1, waiting for transfers between devices, body(): lax.psum(mlp_part, 'tensor') + reduce_bias.astype(jnp.float32)  216 us
    psum x1, waiting for transfers between devices, body(): lax.psum(hidden_two_part, 'tensor')  128 us
    psum x1, waiting for transfers between devices, body(): lax.psum(attention_part, 'tensor') + output_bias.astype(jnp.float32)  119 us
    unnamed x160, local copies, waits for them, and re-layouts  36.1 us
    psum x1, blocking collectives, body(): lax.psum((modulate_weight_grad, modulate_bias_grad, input_weight_grad, in...  24.9 us
    reduce_sum x2, other arithmetic, norm_back(): mean_grad = jnp.mean(grad_norm, axis=-1, keepdims=True)  24 us
    reduce_sum x1, other arithmetic, body(): scale_two_grad = jnp.sum(hidden_two_grad * normed_two, axis=1)  22.4 us
  transfers between devices with their start and end apart: 7, of which 6 were waited for; matrix products, arithmetic and copies ran while one was open for 9% of the time, Pallas kernels for 0%

profile of v1, /device:TPU:0, one launch (start us, length us, event | category | flops | bytes accessed | tf_op | source)
XLA Modules:
  0.0 1089.6 jit_solution(335831073917692594)
XLA Ops:
  7.3 0.8 convert_element_type.99
  8.1 0.7 copy-done
  8.8 1.8 convolution_add_fusion
  10.6 3.3 collective-permute-start
  13.9 0.7 convert_element_type.108
  14.6 3.1 convert_reduce_fusion.2
  17.7 1.4 multiply_reduce_fusion.5
  19.3 0.8 fusion.68
  20.9 3.7 collective-permute-done.1
  25.6 4.1 collective-permute-done.2
  30.1 4.8 fusion.17
  35.2 0.8 multiply_reduce_fusion.7
  36.0 0.8 exponential_reduce_fusion
  36.8 2.0 multiply_convert_fusion.3
  39.1 5.3 fusion.71
  45.7 4.5 copy.86
  50.1 2.2 convert_reduce_fusion
  52.3 4.9 broadcast_multiply_fusion
  57.2 2.7 copy.61
  60.0 4.4 copy.87
  64.3 118.9 %all-reduce.8.cloned.1.call-done = f32[2048,1152]{1,0:T(8,128)} async-done(((f32[2048,1152]{1,0:T(8,128)}), f32[2048,1152]{1,0:T(8,128)}) %all-reduce.8.cloned.1.call-update) | async-done | bytes 9437200 | tf_op jit(solution)/shard_map/psum | solution.py:124
  183.2 10.4 fusion.64
  193.6 4.9 multiply_reduce_fusion.4
  198.5 1.4 copy-done.2
  199.9 2.2 fusion.5
  202.3 0.7 slice-done.13
  203.6 9.3 multiply_convert_fusion
  212.9 1.4 copy-done.56
  214.3 6.6 fusion.73
  221.0 10.0 fusion.72
  230.9 128.1 %all-reduce.10.cloned.1.call-done = f32[2048,1152]{1,0:T(8,128)} async-done(((f32[2048,1152]{1,0:T(8,128)}), f32[2048,1152]{1,0:T(8,128)}) %all-reduce.10.cloned.1.call-update) | async-done | bytes 9437200 | tf_op jit(solution)/shard_map/psum | solution.py:161
  359.1 8.1 fusion.9
  367.2 1.0 copy-done.6
  368.2 10.7 convert_reduce_fusion.1
  378.9 2.6 multiply_reduce_fusion.8
  381.5 1.3 copy-done.5
  382.8 1.0 convolution_convert_fusion
  383.8 1.3 multiply_reduce_fusion.6
  385.2 1.2 multiply_convert_fusion.1
  386.3 0.8 fusion.27
  387.7 2.1 fusion.57
  390.0 5.3 convolution_bitcast_fusion
  396.0 7.9 fusion.76
  404.0 4.7 fusion.75
  408.8 4.3 fusion.74
  413.1 6.6 fusion.22
  419.7 215.8 %all-reduce.12.cloned.1.call-done = (f32[2048,1152]{1,0:T(8,128)}, f32[2048,1152]{1,0:T(8,128)}) async-done(((f32[2048,1152]{1,0:T(8,128)}, f32[2048,1152]{1,0:T(8,128)}), (f32[2048,1152]{1,0:T(8,128)}, f32[2048,1152]{1,0:T(8,128)})) %all-reduce.12.cloned.1.call-update) | async-done | bytes 18874384 | tf_op jit(solution)/shard_map/psum | solution.py:145
  635.5 22.4 %fusion.7 = (f32[8,1152]{1,0:T(8,128)S(1)}, f32[8,1152]{1,0:T(8,128)S(1)}, f32[8,1152]{1,0:T(8,128)S(1)}, f32[8,1152]{1,0:T(8,128)S(1)}, f32[8,1152]{1,0:T(8,128...) fusion(f32[2048,1152]{1,0:T(8,128)} %all-reduce.10.cloned.1.call-done, f32[2048,1152]{1,0:T(8,128)} %all-reduce.8.cloned.1.call-done, ...), kind=kLoop, calls=%fused_computation.17 | loop fusion | flops 61286400 | bytes 56976384 | tf_op jit(solution)/shard_map/reduce_sum | solution.py:165
  658.0 3.8 fusion.37
  661.8 4.6 copy.88
  666.4 5.8 fusion.21
  672.4 1.8 slice_reduce_fusion.1
  674.6 15.9 %fusion.8 = (f32[2048]{0:T(1024)S(1)}, f32[2048]{0:T(1024)S(1)}, f32[2048,1152]{1,0:T(8,128)}) fusion(f32[2048,1152]{1,0:T(8,128)} %get-tuple-element.31, f32[8,1152]{1,0:T(8,128)S(1)} %get-tuple-element.67, f32[2048]{0:T(1024)S(1)} %copy-done.29, f32[2048]{0:T(1024)S(1)} %copy-done.27, bf16[2048,1152]{1,0:T(8,128)(2,1)} %param.17, ...), kind=kLoop, calls=%fused_computation.34 | loop fusion | flops 21229568 | bytes 42573824 | tf_op jit(solution)/shard_map/reduce_sum | solution.py:18
  690.6 1.7 slice-done.1
  692.3 1.2 slice-done.3
  693.7 1.3 slice-done.8
  695.2 5.3 multiply_add_fusion
  700.6 24.9 %all-reduce.1 = (f32[6,144]{1,0:T(8,128)}, f32[2,144]{1,0:T(2,128)}, f32[1152]{0:T(1024)}, f32[576]{0:T(1024)}, f32[1152]{0:T(1024)}, /*index=5*/f32[1152,2,2]{0,2,1:T(2,128)}, f32[2,2]{1,0:T(2,128)}) all-reduce(f32[6,144]{1,0:T(8,128)S(1)} %dynamic-slice_reduce_fusion, ...), channel_id=1, replica_groups=mesh['dp'=4,'tensor'=8] {'dp'}, use_global_device_ids=true, to_apply=%region_23.24 | all-reduce | flops 8644 | bytes 69152 | tf_op jit(solution)/shard_map/psum | solution.py:246
  725.6 347.4 %all-reduce.14.cloned.1.call-done = (f32[1152,6,144]{0,2,1:T(8,128)}, f32[1152,3,144]{0,2,1:T(8,128)}, f32[144,1152]{1,0:T(8,128)}, f32[1152,576]{0,1:T(8,128)}, f32[576,1152]{1,0:T(8,128)}) async-done(((f32[1152,6,144]{0,2,1:T(8,128)}, f32[1152,3,144]{0,2,1:T(8,128)}, f32[144,1152]{1,0:T(8,128)}, f32[1152,576]{0,1:T(8,128)}, f32[576,1152]{1,0:T(8,128)}), (f32[1152,6,144]{0,2,1:T(8,128)}, ...) | async-done | bytes 11943952 | tf_op jit(solution)/shard_map/psum | solution.py:246
  1073.0 4.5 copy.106
  1077.4 1.3 copy.107
  1078.7 0.8 copy.108
  1079.6 1.5 copy.109
  1081.1 1.5 copy.110
  (204 shorter events, 7.5 us)
Async XLA Ops:
  7.2 176.0 %all-reduce.8.cloned.1.call-start = ((), (), s32[]{:S(2)}) async-start(), calls=%async_computation | async-start | bytes 18874368 | tf_op jit(solution)/shard_map/psum | solution.py:124
  7.2 10.5 copy-start.3
  10.6 9.6 collective-permute-start
  14.6 4.6 copy-start.24
  14.6 4.6 copy-start.53
  14.6 4.7 copy-start.52
  14.6 4.7 copy-start.54
  14.6 6.3 copy-start.47
  14.6 15.5 %copy-start.50 = (bf16[1152,3,144]{0,2,1:T(8,128)(2,1)S(1)}, bf16[1152,3,144]{0,2,1:T(8,128)(2,1)}, u32[]{:S(2)}) copy-start(bf16[1152,3,144]{0,2,1:T(8,128)(2,1)} %param.23) | copy-start | bytes 2985988
  17.7 7.8 copy-start.26
  20.1 5.4 copy-start.28
  20.2 4.4 collective-permute-start.1
  20.9 14.0 %copy-start.31 = (f32[8,256]{1,0:T(8,128)}, f32[8,256]{1,0:T(8,128)S(1)}, u32[]{:S(2)}) copy-start(f32[8,256]{1,0:T(8,128)S(1)} %div.41) | copy-start | bytes 24580
  24.7 4.9 collective-permute-start.2
  25.4 11.4 %copy-start.38 = (f32[2,72]{1,0:T(2,128)}, f32[2,72]{1,0:T(2,128)S(1)}, u32[]{:S(2)}) copy-start(f32[2,72]{1,0:T(2,128)S(1)} %add.219) | copy-start | bytes 1732
  25.5 9.7 copy-start.36
  25.6 9.3 copy-start.33
  39.1 5.4 copy-start.8
  44.5 314.6 %all-reduce.10.cloned.1.call-start = ((), (), s32[]{:S(2)}) async-start(), calls=%async_computation.1 | async-start | bytes 18874368 | tf_op jit(solution)/shard_map/psum | solution.py:161
  45.3 4.9 slice-start.5
  45.6 4.5 slice-start.6
  52.3 4.9 copy-start.12
  193.6 6.4 copy-start.2
  193.6 8.6 slice-start.12
  193.6 8.7 slice-start.14
  199.9 3.2 slice-start.15
  199.9 3.7 copy-start.48
  202.1 10.7 copy-start.14
  220.9 414.6 %all-reduce.12.cloned.1.call-start = ((), (), s32[]{:S(2)}) async-start(), calls=%async_computation.2 | async-start | bytes 37748736 | tf_op jit(solution)/shard_map/psum | solution.py:145
  359.1 9.1 copy-start.6
  368.2 10.7 copy-start.13
  378.9 4.9 copy-start.7
  378.9 3.9 copy-start.5
  383.8 3.9 copy-start.17
  395.3 8.6 slice-start.10
  395.3 677.6 %all-reduce.14.cloned.1.call-start = ((), (), s32[]{:S(2)}) async-start(), calls=%async_computation.3 | async-start | bytes 23887872 | tf_op jit(solution)/shard_map/psum | solution.py:246
  396.0 7.9 slice-start.11
  396.0 7.9 copy-start.55
  404.0 4.8 copy-start.9
  408.7 4.3 copy-start.18
  408.7 4.3 copy-start.20
  408.7 4.3 copy-start.32
  408.7 4.3 copy-start.34
  635.5 22.4 %copy-start.25 = (f32[8,1152]{1,0:T(8,128)S(1)}, f32[8,1152]{1,0:T(8,128)}, u32[]{:S(2)}) copy-start(f32[8,1152]{1,0:T(8,128)} %param.18) | copy-start | bytes 110596
  666.4 6.0 copy-start.35
  666.4 7.9 copy-start.45
  666.4 7.9 copy-start.46
  666.4 8.2 copy-start.27
  666.4 8.2 copy-start.29
  666.4 24.1 %slice-start = ((s8[4718592]{0:T(1024)(128)(4,1)}), s8[524288]{0:T(1024)(128)(4,1)S(1)}, s32[]{:S(2)}) async-start(s8[4718592]{0:T(1024)(128)(4,1)} %bitcast.215), calls=%async_computation.4 | async-start | bytes 1048576
  674.6 16.0 %slice-start.2 = ((s8[9437184]{0:T(1024)(128)(4,1)}), s8[4194304]{0:T(1024)(128)(4,1)S(1)}, s32[]{:S(2)}) async-start(s8[9437184]{0:T(1024)(128)(4,1)} %bitcast.217), calls=%async_computation.6 | async-start | bytes 8388608
  674.6 16.0 %slice-start.7 = ((s8[9437184]{0:T(1024)(128)(4,1)}), s8[4194304]{0:T(1024)(128)(4,1)S(1)}, s32[]{:S(2)}) async-start(s8[9437184]{0:T(1024)(128)(4,1)} %bitcast.222), calls=%async_computation.11 | async-start | bytes 8388608
  674.6 17.7 %slice-start.1 = ((s8[4718592]{0:T(1024)(128)(4,1)}), s8[4194304]{0:T(1024)(128)(4,1)S(1)}, s32[]{:S(2)}) async-start(s8[4718592]{0:T(1024)(128)(4,1)} %bitcast.215), calls=%async_computation.5 | async-start | bytes 8388608
  674.6 18.8 %slice-start.3 = ((s8[9437184]{0:T(1024)(128)(4,1)}), s8[4194304]{0:T(1024)(128)(4,1)S(1)}, s32[]{:S(2)}) async-start(s8[9437184]{0:T(1024)(128)(4,1)} %bitcast.217), calls=%async_computation.7 | async-start | bytes 8388608
  674.6 19.1 %slice-start.4 = ((s8[9437184]{0:T(1024)(128)(4,1)}), s8[1048576]{0:T(1024)(128)(4,1)S(1)}, s32[]{:S(2)}) async-start(s8[9437184]{0:T(1024)(128)(4,1)} %bitcast.217), calls=%async_computation.8 | async-start | bytes 2097152
  674.6 20.3 %slice-start.8 = ((s8[9437184]{0:T(1024)(128)(4,1)}), s8[4194304]{0:T(1024)(128)(4,1)S(1)}, s32[]{:S(2)}) async-start(s8[9437184]{0:T(1024)(128)(4,1)} %bitcast.222), calls=%async_computation.12 | async-start | bytes 8388608
  674.6 20.5 %slice-start.9 = ((s8[9437184]{0:T(1024)(128)(4,1)}), s8[1048576]{0:T(1024)(128)(4,1)S(1)}, s32[]{:S(2)}) async-start(s8[9437184]{0:T(1024)(128)(4,1)} %bitcast.222), calls=%async_computation.13 | async-start | bytes 2097152
  695.2 5.5 copy-start.30
  695.2 5.5 copy-start.42
  1073.0 4.5 copy-start.21
  1073.0 5.8 copy-start.23
  1073.0 6.6 copy-start.16
  1077.4 3.6 copy-start.15
  1078.7 3.9 copy-start.1
  (16 other events, 27.8 us)
Sparse Core Ops, SparseCore 0:
  44.6 138.5 all-reduce.7
  221.1 137.9 all-reduce.9
  395.5 239.9 all-reduce.11
  661.9 410.9 all-reduce.13
